TPU v7x, 32 devices: a whole 2x2x4 slice. The times are simulated.
32 devices in a mesh: replica: 4 (over y, x), fsdp: 8 (over z, core).
Axes of the slice: x: 2, y: 2, z: 4, core: 2. Of those that a mesh axis runs over, the one named last changes fastest.
Arguments:
- latents: bfloat16 [32, 256, 1152], P(('replica', 'fsdp')), may hold values from -6 to 6
- condition: bfloat16 [32, 1152], P(('replica', 'fsdp')), may hold values from -6 to 6
- bucket: int32 [32], P(('replica', 'fsdp')), may hold values from 0 to 2, as said below
- keep_slots: int32 [32, 128], P(('replica', 'fsdp')), may hold values from 0 to 255, as said below
- modulation_weight: bfloat16 [1152, 6912], P('fsdp'), may hold values from -0.1875 to 0.1875
- modulation_bias: bfloat16 [6912], P('fsdp'), may hold values from -1.5 to 1.5
- projection_weight: bfloat16 [1152, 3456], P('fsdp'), may hold values from -0.1875 to 0.1875
- query_value_bias: bfloat16 [2304], P('fsdp'), may hold values from -1.5 to 1.5
- output_weight: bfloat16 [1152, 1152], P('fsdp'), may hold values from -0.75 to 0.75
- output_bias: bfloat16 [1152], P('fsdp'), may hold values from -1.5 to 1.5
- expand_weight: bfloat16 [1152, 4608], P('fsdp'), may hold values from -0.1875 to 0.1875
- expand_bias: bfloat16 [4608], P('fsdp'), may hold values from -2.5 to 2.5
- reduce_weight: bfloat16 [4608, 1152], P('fsdp'), may hold values from -0.125 to 0.125
- reduce_bias: bfloat16 [1152], P('fsdp'), may hold values from -1.5 to 1.5
- cotangent: bfloat16 [32, 256, 1152], P(('replica', 'fsdp')), may hold values from -6 to 6
Outputs:
- block_out: bfloat16 [32, 256, 1152], P(('replica', 'fsdp'))
- grad_latents: bfloat16 [32, 256, 1152], P(('replica', 'fsdp'))
- grad_condition: float32 [32, 1152], P(('replica', 'fsdp'))
- grad_modulation_weight: float32 [1152, 6912], P('fsdp')
- grad_modulation_bias: float32 [6912], P('fsdp')
- grad_projection_weight: float32 [1152, 3456], P('fsdp')
- grad_query_value_bias: float32 [2304], P('fsdp')
- grad_output_weight: float32 [1152, 1152], P('fsdp')
- grad_output_bias: float32 [1152], P('fsdp')
- grad_expand_weight: float32 [1152, 4608], P('fsdp')
- grad_expand_bias: float32 [4608], P('fsdp')
- grad_reduce_weight: float32 [4608, 1152], P('fsdp')
- grad_reduce_bias: float32 [1152], P('fsdp')
Inputs may be any that keep to these rules, and one draw needn't show every extreme that they name: `bucket`: 0 marks a 16 x 16 grid of tokens, 1 and 2 grids of (12) x (20) and (20) x (12); an image's real tokens fill its first slots, the rest are padding. `keep_slots`: each row holds distinct slots of that image's real tokens in random order; the first live_count entries are the kept tokens, the others of the image are routed past the block.
All inputs are finite; a program needn't handle non-finite values.
Results may differ from a plain program's by a relative error of at most 0.02.
Values may be sent and summed in bfloat16 or wider, within the bound.
A program may use at most 256 MiB of HBM per device.

v0:
```python
import jax
import jax.numpy as jnp
from jax import lax
from jax.sharding import PartitionSpec as P

HEADS = 16
HEAD_DIM = 72


def layer_norm(rows_in):
    row_mean = jnp.mean(rows_in, axis=-1, keepdims=True)
    centred = rows_in - row_mean
    row_var = jnp.mean(centred * centred, axis=-1, keepdims=True)
    return centred * lax.rsqrt(row_var + 1e-06)


def modulate(rows_in, shift_part, scale_part):
    return layer_norm(rows_in) * (1.0 + scale_part) + shift_part


def gelu_tanh(values_in):
    return jax.nn.gelu(values_in, approximate=True)


def place_rows(target_rows, target_index, new_rows):
    return target_rows.at[target_index].set(new_rows, mode="drop")


def column_sums(rows_in):
    return jnp.sum(rows_in.astype(jnp.float32), axis=0)


def local(
    latents,
    condition,
    bucket,
    keep_slots,
    modulation_weight,
    modulation_bias,
    projection_weight,
    query_value_bias,
    output_weight,
    output_bias,
    expand_weight,
    expand_bias,
    reduce_weight,
    reduce_bias,
    cotangent,
):
    f32 = jnp.float32
    bf16 = jnp.bfloat16
    images, slot_count, model_width = latents.shape
    kept_rows = keep_slots.shape[1]
    row_count = images * kept_rows
    score_scale = HEAD_DIM ** (-0.5)
    shape_heads = (images, kept_rows, HEADS, HEAD_DIM)
    (
        full_mod_w,
        full_mod_b,
        full_proj_w,
        full_qv_b,
        full_out_w,
        full_out_b,
        full_exp_w,
        full_exp_b,
        full_red_w,
        full_red_b,
    ) = (
        lax.all_gather(modulation_weight, "fsdp", axis=0, tiled=True),
        lax.all_gather(modulation_bias, "fsdp", axis=0, tiled=True),
        lax.all_gather(projection_weight, "fsdp", axis=0, tiled=True),
        lax.all_gather(query_value_bias, "fsdp", axis=0, tiled=True),
        lax.all_gather(output_weight, "fsdp", axis=0, tiled=True),
        lax.all_gather(output_bias, "fsdp", axis=0, tiled=True),
        lax.all_gather(expand_weight, "fsdp", axis=0, tiled=True),
        lax.all_gather(expand_bias, "fsdp", axis=0, tiled=True),
        lax.all_gather(reduce_weight, "fsdp", axis=0, tiled=True),
        lax.all_gather(reduce_bias, "fsdp", axis=0, tiled=True),
    )
    live_count = jnp.where(bucket == 0, slot_count, slot_count - 16) // 2
    live_rows = jnp.arange(kept_rows, dtype=jnp.int32)[None, :] < live_count[:, None]
    live_float = live_rows.astype(f32)[:, :, None]
    gather_index = keep_slots[:, :, None]
    kept = jnp.take_along_axis(latents, gather_index, axis=1).astype(f32)
    cond_float = condition.astype(f32)
    cond_act = jax.nn.silu(cond_float).astype(bf16)
    modulation = jnp.dot(cond_act, full_mod_w, preferred_element_type=f32) + full_mod_b.astype(f32)
    pieces = [modulation[:, None, i * model_width : (i + 1) * model_width] for i in range(6)]
    shift_attn, scale_attn, gate_attn, shift_mlp, scale_mlp, gate_mlp = pieces
    normed_one = modulate(kept, shift_attn, scale_attn).astype(bf16).reshape(row_count, model_width)
    projected = jnp.dot(normed_one, full_proj_w, preferred_element_type=f32)
    bias_qv = full_qv_b.astype(f32)
    query_rows = (
        (projected[:, :model_width] + bias_qv[:model_width]).astype(bf16).reshape(shape_heads)
    )
    key_rows = projected[:, model_width : 2 * model_width].astype(bf16).reshape(shape_heads)
    value_rows = (
        (projected[:, 2 * model_width :] + bias_qv[model_width:]).astype(bf16).reshape(shape_heads)
    )

    def masked_scores(queries, keys_in):
        raw = (
            jnp.einsum("bqhd,bkhd->bhqk", queries, keys_in, preferred_element_type=f32)
            * score_scale
        )
        return jnp.where(live_rows[:, None, None, :], raw, -1e30)

    scores = masked_scores(query_rows, key_rows)
    row_max = jnp.max(scores, axis=-1, keepdims=True)
    row_total = jnp.sum(jnp.exp(scores - row_max), axis=-1, keepdims=True)
    log_total = row_max + jnp.log(row_total)
    probs = jnp.exp(scores - log_total)
    attended = (
        jnp.einsum("bhqk,bkhd->bqhd", probs.astype(bf16), value_rows, preferred_element_type=f32)
        .astype(bf16)
        .reshape(row_count, model_width)
    )
    branch_attn = (
        jnp.dot(attended, full_out_w, preferred_element_type=f32) + full_out_b.astype(f32)
    ).reshape(images, kept_rows, model_width)
    mixed = kept + gate_attn * branch_attn
    normed_two = modulate(mixed, shift_mlp, scale_mlp).astype(bf16).reshape(row_count, model_width)
    hidden = jnp.dot(normed_two, full_exp_w, preferred_element_type=f32) + full_exp_b.astype(f32)
    activation = gelu_tanh(hidden).astype(bf16)
    branch_mlp = (
        jnp.dot(activation, full_red_w, preferred_element_type=f32) + full_red_b.astype(f32)
    ).reshape(images, kept_rows, model_width)
    result = mixed + gate_mlp * branch_mlp
    target = jnp.where(live_rows, keep_slots, slot_count)
    block_out = jax.vmap(place_rows)(latents, target, result.astype(bf16))
    back_mod_w, back_proj_w, back_out_w, back_exp_w, back_red_w = (
        lax.all_gather(modulation_weight, "fsdp", axis=0, tiled=True),
        lax.all_gather(projection_weight, "fsdp", axis=0, tiled=True),
        lax.all_gather(output_weight, "fsdp", axis=0, tiled=True),
        lax.all_gather(expand_weight, "fsdp", axis=0, tiled=True),
        lax.all_gather(reduce_weight, "fsdp", axis=0, tiled=True),
    )
    grad_rows = jnp.take_along_axis(cotangent, gather_index, axis=1).astype(f32) * live_float
    grad_gate_mlp = jnp.sum(grad_rows * branch_mlp, axis=1)
    grad_mlp = (gate_mlp * grad_rows).astype(bf16).reshape(row_count, model_width)
    local_red_w = jnp.einsum("rm,rd->md", activation, grad_mlp, preferred_element_type=f32)
    local_red_b = column_sums(grad_mlp)
    grad_act = jnp.einsum("rd,md->rm", grad_mlp, back_red_w, preferred_element_type=f32)
    gelu_pull = jax.vjp(gelu_tanh, hidden)[1]
    grad_hidden = gelu_pull(grad_act)[0].astype(bf16)
    local_exp_w = jnp.einsum("rd,rm->dm", normed_two, grad_hidden, preferred_element_type=f32)
    local_exp_b = column_sums(grad_hidden)
    mlp_red_w, mlp_red_b, mlp_exp_w, mlp_exp_b = (
        lax.psum_scatter(
            local_red_w.astype(jnp.bfloat16), "fsdp", scatter_dimension=0, tiled=True
        ).astype(jnp.float32),
        lax.psum_scatter(
            local_red_b.astype(jnp.bfloat16), "fsdp", scatter_dimension=0, tiled=True
        ).astype(jnp.float32),
        lax.psum_scatter(
            local_exp_w.astype(jnp.bfloat16), "fsdp", scatter_dimension=0, tiled=True
        ).astype(jnp.float32),
        lax.psum_scatter(
            local_exp_b.astype(jnp.bfloat16), "fsdp", scatter_dimension=0, tiled=True
        ).astype(jnp.float32),
    )
    grad_normed_two = jnp.einsum(
        "rm,dm->rd", grad_hidden, back_exp_w, preferred_element_type=f32
    ).reshape(images, kept_rows, model_width)
    pull_two = jax.vjp(modulate, mixed, shift_mlp, scale_mlp)[1]
    grad_mixed_ln, grad_shift_mlp, grad_scale_mlp = pull_two(grad_normed_two)
    grad_mixed = grad_rows + grad_mixed_ln
    grad_gate_attn = jnp.sum(grad_mixed * branch_attn, axis=1)
    grad_attn = (gate_attn * grad_mixed).astype(bf16).reshape(row_count, model_width)
    local_out_w = jnp.einsum("rd,re->de", attended, grad_attn, preferred_element_type=f32)
    local_out_b = column_sums(grad_attn)
    grad_attended = (
        jnp.einsum("re,de->rd", grad_attn, back_out_w, preferred_element_type=f32)
        .astype(bf16)
        .reshape(shape_heads)
    )
    scores_again = masked_scores(query_rows, key_rows)
    probs_again = jnp.exp(scores_again - log_total)
    grad_values = jnp.einsum(
        "bhqk,bqhd->bkhd", probs_again.astype(bf16), grad_attended, preferred_element_type=f32
    ).astype(bf16)
    grad_probs = jnp.einsum(
        "bqhd,bkhd->bhqk", grad_attended, value_rows, preferred_element_type=f32
    )
    row_inner = jnp.sum(grad_probs * probs_again, axis=-1, keepdims=True)
    grad_scores = (probs_again * (grad_probs - row_inner)).astype(bf16)
    grad_query = (
        jnp.einsum("bhqk,bkhd->bqhd", grad_scores, key_rows, preferred_element_type=f32)
        * score_scale
    ).astype(bf16)
    grad_keys = (
        jnp.einsum("bhqk,bqhd->bkhd", grad_scores, query_rows, preferred_element_type=f32)
        * score_scale
    ).astype(bf16)
    grad_projected = jnp.concatenate(
        [
            grad_query.reshape(row_count, model_width),
            grad_keys.reshape(row_count, model_width),
            grad_values.reshape(row_count, model_width),
        ],
        axis=1,
    )
    local_proj_w = jnp.einsum("rd,re->de", normed_one, grad_projected, preferred_element_type=f32)
    local_qv_b = jnp.concatenate(
        [
            column_sums(grad_projected[:, :model_width]),
            column_sums(grad_projected[:, 2 * model_width :]),
        ]
    )
    grad_normed_one = jnp.einsum(
        "re,de->rd", grad_projected, back_proj_w, preferred_element_type=f32
    ).reshape(images, kept_rows, model_width)
    pull_one = jax.vjp(modulate, kept, shift_attn, scale_attn)[1]
    grad_kept_ln, grad_shift_attn, grad_scale_attn = pull_one(grad_normed_one)
    grad_kept = grad_mixed + grad_kept_ln
    grad_latents = jax.vmap(place_rows)(cotangent, target, grad_kept.astype(bf16))
    grad_modulation = jnp.concatenate(
        [
            grad_shift_attn[:, 0],
            grad_scale_attn[:, 0],
            grad_gate_attn,
            grad_shift_mlp[:, 0],
            grad_scale_mlp[:, 0],
            grad_gate_mlp,
        ],
        axis=1,
    ).astype(bf16)
    grad_cond_act = jnp.einsum("be,de->bd", grad_modulation, back_mod_w, preferred_element_type=f32)
    silu_pull = jax.vjp(jax.nn.silu, cond_float)[1]
    grad_condition = silu_pull(grad_cond_act)[0]
    local_mod_w = jnp.einsum("bd,be->de", cond_act, grad_modulation, preferred_element_type=f32)
    local_mod_b = column_sums(grad_modulation)
    rest_mod_w, rest_mod_b, rest_proj_w, rest_qv_b, rest_out_w, rest_out_b = (
        lax.psum_scatter(
            local_mod_w.astype(jnp.bfloat16), "fsdp", scatter_dimension=0, tiled=True
        ).astype(jnp.float32),
        lax.psum_scatter(
            local_mod_b.astype(jnp.bfloat16), "fsdp", scatter_dimension=0, tiled=True
        ).astype(jnp.float32),
        lax.psum_scatter(
            local_proj_w.astype(jnp.bfloat16), "fsdp", scatter_dimension=0, tiled=True
        ).astype(jnp.float32),
        lax.psum_scatter(
            local_qv_b.astype(jnp.bfloat16), "fsdp", scatter_dimension=0, tiled=True
        ).astype(jnp.float32),
        lax.psum_scatter(
            local_out_w.astype(jnp.bfloat16), "fsdp", scatter_dimension=0, tiled=True
        ).astype(jnp.float32),
        lax.psum_scatter(
            local_out_b.astype(jnp.bfloat16), "fsdp", scatter_dimension=0, tiled=True
        ).astype(jnp.float32),
    )
    shares = (
        lax.psum_scatter(
            rest_mod_w.astype(jnp.bfloat16), "replica", scatter_dimension=1, tiled=True
        ).astype(jnp.float32),
        lax.psum_scatter(
            rest_proj_w.astype(jnp.bfloat16), "replica", scatter_dimension=1, tiled=True
        ).astype(jnp.float32),
        lax.psum_scatter(
            rest_out_w.astype(jnp.bfloat16), "replica", scatter_dimension=1, tiled=True
        ).astype(jnp.float32),
        lax.psum_scatter(
            mlp_exp_w.astype(jnp.bfloat16), "replica", scatter_dimension=1, tiled=True
        ).astype(jnp.float32),
        lax.psum_scatter(
            mlp_red_w.astype(jnp.bfloat16), "replica", scatter_dimension=1, tiled=True
        ).astype(jnp.float32),
    )
    sum_mod_w, sum_proj_w, sum_out_w, sum_exp_w, sum_red_w = (
        lax.all_gather(shares[0].astype(jnp.bfloat16), "replica", axis=1, tiled=True).astype(
            jnp.float32
        ),
        lax.all_gather(shares[1].astype(jnp.bfloat16), "replica", axis=1, tiled=True).astype(
            jnp.float32
        ),
        lax.all_gather(shares[2].astype(jnp.bfloat16), "replica", axis=1, tiled=True).astype(
            jnp.float32
        ),
        lax.all_gather(shares[3].astype(jnp.bfloat16), "replica", axis=1, tiled=True).astype(
            jnp.float32
        ),
        lax.all_gather(shares[4].astype(jnp.bfloat16), "replica", axis=1, tiled=True).astype(
            jnp.float32
        ),
    )
    sum_mod_b, sum_qv_b, sum_out_b, sum_exp_b, sum_red_b = lax.psum(
        (rest_mod_b, rest_qv_b, rest_out_b, mlp_exp_b, mlp_red_b), "replica"
    )
    return (
        block_out,
        grad_latents,
        grad_condition,
        sum_mod_w,
        sum_mod_b,
        sum_proj_w,
        sum_qv_b,
        sum_out_w,
        sum_out_b,
        sum_exp_w,
        sum_exp_b,
        sum_red_w,
        sum_red_b,
    )


def solution(mesh):
    placed = (
        P(("replica", "fsdp"), None, None),
        P(("replica", "fsdp"), None),
        P(("replica", "fsdp")),
        P(("replica", "fsdp"), None),
        P("fsdp", None),
        P("fsdp"),
        P("fsdp", None),
        P("fsdp"),
        P("fsdp", None),
        P("fsdp"),
        P("fsdp", None),
        P("fsdp"),
        P("fsdp", None),
        P("fsdp"),
        P(("replica", "fsdp"), None, None),
    )
    return jax.shard_map(
        local,
        mesh=mesh,
        in_specs=placed,
        out_specs=(
            P(("replica", "fsdp"), None, None),
            P(("replica", "fsdp"), None, None),
            P(("replica", "fsdp"), None),
            P("fsdp", None),
            P("fsdp"),
            P("fsdp", None),
            P("fsdp"),
            P("fsdp", None),
            P("fsdp"),
            P("fsdp", None),
            P("fsdp"),
            P("fsdp", None),
            P("fsdp"),
        ),
        check_vma=False,
    )
```

profile of v0, /device:TPU:0, one launch (start us, length us, event | category | flops | bytes accessed | tf_op | source)
XLA Modules:
  0.0 1305.8 jit_solution(7844802750100305167)
XLA Ops:
  17.3 32.9 %all-reduce.12 = (bf16[2304]{0:T(1024)(128)(2,1)S(1)}, bf16[6912]{0:T(1024)(128)(2,1)S(1)}, bf16[4608]{0:T(1024)(128)(2,1)S(1)}, bf16[1152]{0:T(1024)(128)(2,1)S(1)}, bf16[1152]{0:T(1024)(128)(2,1)S(1)}) all-reduce(bf16[2304]{0:T(1024)(128)(2,1)S(1)} %dynamic-update-slice.1, ...), channel_id=1, replica_groups=mesh['replica'=4,'fsdp'=8] {'fsdp'}, use_global_device_ids=true, to_apply=%add.1 | all-reduce | flops 16128 | bytes 64512
  53.1 104.4 %all-gather.12.cloned.1.call-done = bf16[1152,6912]{1,0:T(8,128)(2,1)} async-done(((bf16[144,6912]{1,0:T(8,128)(2,1)}), bf16[1152,6912]{1,0:T(8,128)(2,1)}) %all-gather.12.cloned.1.call-update) | async-done | bytes 15925264 | tf_op jit(solution)/shard_map/all_gather | solution.py:69
  157.5 7.7 convolution_reduce_fusion
  165.4 70.6 %all-gather.14.cloned.1.call-done = bf16[1152,3456]{1,0:T(8,128)(2,1)} async-done(((bf16[144,3456]{1,0:T(8,128)(2,1)}), bf16[1152,3456]{1,0:T(8,128)(2,1)}) %all-gather.14.cloned.1.call-update) | async-done | bytes 7962640 | tf_op jit(solution)/shard_map/all_gather | solution.py:71
  236.0 4.7 fusion.65
  244.9 25.5 %all-gather.16.cloned.1.call-done = bf16[1152,1152]{1,0:T(8,128)(2,1)} async-done(((bf16[144,1152]{1,0:T(8,128)(2,1)}), bf16[1152,1152]{1,0:T(8,128)(2,1)}) %all-gather.16.cloned.1.call-update) | async-done | bytes 2654224 | tf_op jit(solution)/shard_map/all_gather | solution.py:73
  270.4 3.3 fusion.72
  273.9 97.4 %all-gather.18.cloned.1.call-done = bf16[1152,4608]{1,0:T(8,128)(2,1)} async-done(((bf16[144,4608]{1,0:T(8,128)(2,1)}), bf16[1152,4608]{1,0:T(8,128)(2,1)}) %all-gather.18.cloned.1.call-update) | async-done | bytes 10616848 | tf_op jit(solution)/shard_map/all_gather | solution.py:75
  371.4 7.2 convolution_add_fusion
  378.6 93.2 %all-gather.20.cloned.1.call-done = bf16[4608,1152]{1,0:T(8,128)(2,1)} async-done(((bf16[576,1152]{1,0:T(8,128)(2,1)}), bf16[4608,1152]{1,0:T(8,128)(2,1)}) %all-gather.20.cloned.1.call-update) | async-done | bytes 10616848 | tf_op jit(solution)/shard_map/all_gather | solution.py:77
  471.8 8.6 fusion.77
  481.4 6.0 convolution_convert_fusion.1
  487.4 8.9 convolution_convert_fusion
  496.5 7.9 fusion.25
  515.6 6.9 fusion.76
  523.0 8.0 fusion.24
  532.7 5.8 multiply_convert_fusion
  539.5 3.3 convolution_convert_fusion.3
  542.9 6.8 convolution_convert_fusion.2
  549.8 46.8 %reduce-scatter.27.cloned.1.call-done = bf16[144,4608]{1,0:T(8,128)(2,1)} async-done(((bf16[1152,4608]{1,0:T(8,128)(2,1)}), bf16[144,4608]{1,0:T(8,128)(2,1)}) %reduce-scatter.27.cloned.1.call-update) | async-done | bytes 1327120 | tf_op jit(solution)/shard_map/reduce_scatter | solution.py:155
  596.6 3.8 copy.84
  600.4 107.6 %reduce-scatter.29.cloned.1.call-done = bf16[576,1152]{1,0:T(8,128)(2,1)} async-done(((bf16[4608,1152]{1,0:T(8,128)(2,1)}), bf16[576,1152]{1,0:T(8,128)(2,1)}) %reduce-scatter.29.cloned.1.call-update) | async-done | bytes 1327120 | tf_op jit(solution)/shard_map/reduce_scatter | solution.py:149
  708.0 2.6 copy.86
  710.7 158.8 %reduce-scatter.21.cloned.1.call-done = bf16[144,6912]{1,0:T(8,128)(2,1)} async-done(((bf16[1152,6912]{1,0:T(8,128)(2,1)}), bf16[144,6912]{1,0:T(8,128)(2,1)}) %reduce-scatter.21.cloned.1.call-update) | async-done | bytes 1990672 | tf_op jit(solution)/shard_map/reduce_scatter | solution.py:234
  869.5 4.5 copy.78
  874.1 34.5 %reduce-scatter.25.cloned.1.call-done = bf16[144,1152]{1,0:T(8,128)(2,1)} async-done(((bf16[1152,1152]{1,0:T(8,128)(2,1)}), bf16[144,1152]{1,0:T(8,128)(2,1)}) %reduce-scatter.25.cloned.1.call-update) | async-done | bytes 331792 | tf_op jit(solution)/shard_map/reduce_scatter | solution.py:246
  908.6 2.0 copy.82
  910.7 85.1 %reduce-scatter.23.cloned.1.call-done = bf16[144,3456]{1,0:T(8,128)(2,1)} async-done(((bf16[1152,3456]{1,0:T(8,128)(2,1)}), bf16[144,3456]{1,0:T(8,128)(2,1)}) %reduce-scatter.23.cloned.1.call-update) | async-done | bytes 995344 | tf_op jit(solution)/shard_map/reduce_scatter | solution.py:240
  995.8 2.6 copy.80
  998.4 36.8 %reduce-scatter.37.cloned.1.call-done = bf16[1152,144]{1,0:T(8,128)(2,1)} async-done(((bf16[4608,144]{1,0:T(8,128)(2,1)}), bf16[1152,144]{1,0:T(8,128)(2,1)}) %reduce-scatter.37.cloned.1.call-update) | async-done | bytes 331792
  1037.3 31.1 %reduce-scatter.39.cloned.1.call-done = bf16[288,576]{1,0:T(8,128)(2,1)} async-done(((bf16[1152,576]{1,0:T(8,128)(2,1)}), bf16[288,576]{1,0:T(8,128)(2,1)}) %reduce-scatter.39.cloned.1.call-update) | async-done | bytes 331792
  1068.5 51.1 %reduce-scatter.31.cloned.1.call-done = bf16[1728,144]{1,0:T(8,128)(2,1)} async-done(((bf16[6912,144]{1,0:T(8,128)(2,1)}), bf16[1728,144]{1,0:T(8,128)(2,1)}) %reduce-scatter.31.cloned.1.call-update) | async-done | bytes 497680
  1119.6 2.2 copy.79
  1124.5 2.0 scatter_custom_fusion
  1126.6 2.6 scatter_custom_fusion.1
  1129.4 29.0 %all-reduce.11 = (bf16[6912]{0:T(1024)(128)(2,1)S(1)}, bf16[2304]{0:T(1024)(128)(2,1)S(1)}, bf16[1152]{0:T(1024)(128)(2,1)S(1)}, bf16[4608]{0:T(1024)(128)(2,1)S(1)}, bf16[1152]{0:T(1024)(128)(2,1)S(1)}) all-reduce(bf16[6912]{0:T(1024)(128)(2,1)S(1)} %dynamic-update-slice.10, ...), channel_id=4, replica_groups=mesh['replica'=4,'fsdp'=8] {'fsdp'}, use_global_device_ids=true, to_apply=%region_21.23.clone | all-reduce | flops 16128 | bytes 64512
  1158.7 15.9 %all-reduce.10 = (f32[864]{0:T(1024)}, f32[288]{0:T(512)}, f32[144]{0:T(256)}, f32[576]{0:T(1024)}, f32[144]{0:T(256)}) all-reduce(f32[864]{0:T(1024)S(1)} %dynamic-slice_convert_fusion.1, f32[288]{0:T(512)S(1)} %dynamic-slice_convert_fusion.2, f32[144]{0:T(256)S(1)} %get-tuple-element.86, ...), channel_id=1, replica_groups=mesh['replica'=4,'fsdp'=8] {'replica'}, use_global_device_ids=true, to_apply=%region_22.24 | all-reduce | flops 2016 | bytes 16128 | tf_op jit(solution)/shard_map/psum | solution.py:287
  1174.6 10.6 fusion.50
  1186.3 10.4 all-gather.2
  1199.3 11.5 all-gather.1
  1211.2 2.4 reshape.551
  1213.5 5.5 all-gather.22.cloned.1.call-done
  1219.0 3.1 convert_element_type.254
  1222.1 28.8 %all-gather.24.cloned.1.call-done = bf16[576,1152]{0,1:T(8,128)(2,1)} async-done(((bf16[576,288]{0,1:T(8,128)(2,1)}), bf16[576,1152]{0,1:T(8,128)(2,1)}) %all-gather.24.cloned.1.call-update) | async-done | bytes 1327120 | tf_op jit(solution)/shard_map/all_gather | solution.py:283
  1250.9 2.9 copy.73
  1253.8 34.4 %all-gather.26.cloned.1.call-done = bf16[4,1728,144]{1,2,0:T(8,128)(2,1)} async-done(((bf16[1,1728,144]{1,2,0:T(8,128)(2,1)}), bf16[4,1728,144]{1,2,0:T(8,128)(2,1)}) %all-gather.26.cloned.1.call-update) | async-done | bytes 1990672 | tf_op jit(solution)/shard_map/all_gather | solution.py:271
  1288.2 4.6 copy.69
  1292.8 5.9 reshape.550
  (189 shorter events, 36.5 us)
Async XLA Ops:
  7.2 150.3 %all-gather.12.cloned.1.call-start = ((), (), s32[]{:S(2)}) async-start(), calls=%async_computation.10 | async-start | bytes 17915904 | tf_op jit(solution)/shard_map/all_gather | solution.py:69
  9.4 3.4 copy-start.19
  9.4 6.6 copy-start.29
  9.4 6.9 copy-start.30
  9.4 7.1 copy-start.24
  9.4 7.4 copy-start.20
  9.4 7.6 copy-start.21
  9.5 40.7 %copy-start.31 = (s32[1,128]{1,0:T(1,128)S(1)}, s32[1,128]{1,0:T(1,128)}, u32[]{:S(2)}) copy-start(s32[1,128]{1,0:T(1,128)} %param.20) | copy-start | bytes 1540
  9.5 226.5 %all-gather.14.cloned.1.call-start = ((), (), s32[]{:S(2)}) async-start(), calls=%async_computation.11 | async-start | bytes 8957952 | tf_op jit(solution)/shard_map/all_gather | solution.py:71
  10.2 260.2 %all-gather.16.cloned.1.call-start = ((), (), s32[]{:S(2)}) async-start(), calls=%async_computation.12 | async-start | bytes 2985984 | tf_op jit(solution)/shard_map/all_gather | solution.py:73
  11.0 360.4 %all-gather.18.cloned.1.call-start = ((), (), s32[]{:S(2)}) async-start(), calls=%async_computation.13 | async-start | bytes 11943936 | tf_op jit(solution)/shard_map/all_gather | solution.py:75
  11.5 460.2 %all-gather.20.cloned.1.call-start = ((), (), s32[]{:S(2)}) async-start(), calls=%async_computation.14 | async-start | bytes 11943936 | tf_op jit(solution)/shard_map/all_gather | solution.py:77
  12.1 584.4 %reduce-scatter.27.cloned.1.call-start = ((), (), s32[]{:S(2)}) async-start(), calls=%async_computation.18 | async-start | bytes 11943936 | tf_op jit(solution)/shard_map/reduce_scatter | solution.py:155
  50.2 2.9 copy-start.18
  241.1 3.8 copy-start.9
  242.2 28.2 %copy-start.11 = (bf16[128,1152]{0,1:T(8,128)(2,1)}, bf16[128,1152]{0,1:T(8,128)(2,1)S(1)}, u32[]{:S(2)}) copy-start(bf16[128,1152]{0,1:T(8,128)(2,1)S(1)} %copy.63) | copy-start | bytes 884740
  273.9 104.7 %copy-start.27 = (f32[128]{0:T(128)}, f32[128]{0:T(128)S(1)}, u32[]{:S(2)}) copy-start(f32[128]{0:T(128)S(1)} %multiply_reduce_fusion.1) | copy-start | bytes 1540
  480.4 1.0 copy-start.6
  487.4 220.6 %reduce-scatter.29.cloned.1.call-start = ((), (), s32[]{:S(2)}) async-start(), calls=%async_computation.20 | async-start | bytes 11943936 | tf_op jit(solution)/shard_map/reduce_scatter | solution.py:149
  496.4 373.1 %reduce-scatter.21.cloned.1.call-start = ((), (), s32[]{:S(2)}) async-start(), calls=%async_computation.15 | async-start | bytes 17915904 | tf_op jit(solution)/shard_map/reduce_scatter | solution.py:234
  496.5 8.0 copy-start.28
  504.4 2.9 copy-start.2
  505.5 0.8 copy-start.4
  505.5 3.5 copy-start.22
  512.0 1.8 copy-start.13
  513.5 1.0 copy-start.12
  513.5 1.5 copy-start.10
  514.4 8.0 copy-start.16
  515.0 7.5 copy-start.17
  515.6 6.9 copy-start.15
  515.6 7.4 copy-start.5
  515.6 7.4 copy-start.23
  523.0 8.0 copy-start.26
  523.0 8.0 copy-start.14
  538.5 1.0 copy-start.7
  538.6 370.0 %reduce-scatter.25.cloned.1.call-start = ((), (), s32[]{:S(2)}) async-start(), calls=%async_computation.17 | async-start | bytes 2985984 | tf_op jit(solution)/shard_map/reduce_scatter | solution.py:246
  542.8 452.9 %reduce-scatter.23.cloned.1.call-start = ((), (), s32[]{:S(2)}) async-start(), calls=%async_computation.16 | async-start | bytes 8957952 | tf_op jit(solution)/shard_map/reduce_scatter | solution.py:240
  549.7 485.4 %reduce-scatter.37.cloned.1.call-start = ((), (), s32[]{:S(2)}) async-start(), calls=%async_computation.26 | async-start | bytes 2949120
  600.3 468.0 %reduce-scatter.39.cloned.1.call-start = ((), (), s32[]{:S(2)}) async-start(), calls=%async_computation.27 | async-start | bytes 1843200
  710.6 409.0 %reduce-scatter.31.cloned.1.call-start = ((), (), s32[]{:S(2)}) async-start(), calls=%async_computation.23 | async-start | bytes 4423680
  874.0 311.2 %reduce-scatter.35.cloned.1.call-start = ((), (), s32[]{:S(2)}) async-start(), calls=%async_computation.25 | async-start | bytes 737280
  910.7 287.4 %reduce-scatter.33.cloned.1.call-start = ((), (), s32[]{:S(2)}) async-start(), calls=%async_computation.24 | async-start | bytes 2211840
  998.3 126.1 %copy-start.32 = (s32[1,128]{1,0:T(1,128)S(1)}, s32[1,128]{1,0:T(1,128)}, u32[]{:S(2)}) copy-start(s32[1,128]{1,0:T(1,128)} %param.20) | copy-start | bytes 1540
  998.4 220.6 %all-gather.22.cloned.1.call-start = ((), (), s32[]{:S(2)}) async-start(), calls=%async_computation.19 | async-start | bytes 1658880 | tf_op jit(solution)/shard_map/all_gather | solution.py:280
  1037.2 213.7 %all-gather.24.cloned.1.call-start = ((), (), s32[]{:S(2)}) async-start(), calls=%async_computation.21 | async-start | bytes 1843200 | tf_op jit(solution)/shard_map/all_gather | solution.py:283
  1068.4 219.8 %all-gather.26.cloned.1.call-start = ((), (), s32[]{:S(2)}) async-start(), calls=%async_computation.22 | async-start | bytes 2580480 | tf_op jit(solution)/shard_map/all_gather | solution.py:271
  1126.5 58.7 %copy-start.1 = (bf16[256,1152]{1,0:T(8,128)(2,1)}, bf16[256,1152]{1,0:T(8,128)(2,1)S(1)}, u32[]{:S(2)}) copy-start(bf16[256,1152]{1,0:T(8,128)(2,1)S(1)} %scatter_custom_fusion) | copy-start | bytes 1769476
  1129.1 56.1 %copy-start = (bf16[256,1152]{1,0:T(8,128)(2,1)}, bf16[256,1152]{1,0:T(8,128)(2,1)S(1)}, u32[]{:S(2)}) copy-start(bf16[256,1152]{1,0:T(8,128)(2,1)S(1)} %scatter_custom_fusion.1) | copy-start | bytes 1769476
  (3 other events, 2.1 us)
Sparse Core Ops, SparseCore 0:
  9.7 147.8 all-gather.11
  159.2 76.7 all-gather.13
  237.6 32.7 all-gather.15
  271.9 99.4 all-gather.17
  372.9 98.8 all-gather.19
  487.5 108.9 reduce-scatter.26
  599.0 108.9 reduce-scatter.28
  710.4 159.0 reduce-scatter.20
  872.5 36.0 reduce-scatter.24
  910.9 84.8 reduce-scatter.22
  999.4 35.7 reduce-scatter.36
  1038.0 30.3 reduce-scatter.38
  1072.3 47.2 reduce-scatter.30
  1123.1 25.0 reduce-scatter.34
  1151.7 33.2 reduce-scatter.32
  1187.3 31.6 all-gather.21
  1220.7 30.1 all-gather.23
  1253.2 35.0 all-gather.25
where the time goes:
time: 1310 us
  waiting for transfers between devices  1010 us (77%)
  blocking collectives  99.6 us (8%)
  matrix products  97.2 us (7%)
  local copies, waits for them, and re-layouts  55.6 us (4%)
  between operations  21 us (2%)
  other arithmetic  17.3 us (1%)
    reduce_scatter x1, waiting for transfers between devices, local(): lax.psum_scatter(local_mod_w.astype(jnp.bfloat16), 'fsdp', scatter_dimens...  159 us
    unnamed x23, waiting for transfers between devices  122 us
    reduce_scatter x1, waiting for transfers between devices, local(): lax.psum_scatter(local_red_w.astype(jnp.bfloat16), 'fsdp', scatter_dimens...  108 us
    all_gather x1, waiting for transfers between devices, local(): lax.all_gather(modulation_weight, 'fsdp', axis=0, tiled=True)  104 us
    all_gather x1, waiting for transfers between devices, local(): lax.all_gather(expand_weight, 'fsdp', axis=0, tiled=True)  97.4 us
    all_gather x1, waiting for transfers between devices, local(): lax.all_gather(reduce_weight, 'fsdp', axis=0, tiled=True)  93.2 us
    reduce_scatter x1, waiting for transfers between devices, local(): lax.psum_scatter(local_proj_w.astype(jnp.bfloat16), 'fsdp', scatter_dimen...  85.1 us
    all_gather x1, waiting for transfers between devices, local(): lax.all_gather(projection_weight, 'fsdp', axis=0, tiled=True)  70.6 us
  transfers between devices with their start and end apart: 18, of which 16 were waited for; matrix products, arithmetic and copies ran while one was open for 11% of the time, Pallas kernels for 0%

commit v1 on v0

--- a/solution.py
+++ b/solution.py
@@ -5,6 +5,18 @@
 
 HEADS = 16
 HEAD_DIM = 72
+
+
+def doubled_up(value, axis, dim):
+    ways, here, step = (lax.axis_size(axis), lax.axis_index(axis), value.shape[dim])
+    line, have = (value, 1)
+    while have < ways:
+        line = jnp.concatenate(
+            [line, lax.ppermute(line, axis, [(d, (d - have) % ways) for d in range(ways)])],
+            axis=dim,
+        )
+        have = 2 * have
+    return jnp.roll(line, here * step, axis=dim)
 
 
 def layer_norm(rows_in):
@@ -66,7 +78,7 @@
         full_red_w,
         full_red_b,
     ) = (
-        lax.all_gather(modulation_weight, "fsdp", axis=0, tiled=True),
+        doubled_up(modulation_weight, "fsdp", 0),
         lax.all_gather(modulation_bias, "fsdp", axis=0, tiled=True),
         lax.all_gather(projection_weight, "fsdp", axis=0, tiled=True),
         lax.all_gather(query_value_bias, "fsdp", axis=0, tiled=True),

time: 1310 us -> 1780 us (1.36)
  blocking collectives: 99.6 us -> 596 us
  waiting for transfers between devices: 1010 us -> 948 us
  local copies, waits for them, and re-layouts: 55.6 us -> 85 us
    unnamed x2, blocking collectives: 61.9 us -> 553 us
    ppermute x0 -> x3, waiting for transfers between devices: none -> 189 us  [doubled_up(): lax.ppermute(line, axis, [(d, (d - have) % ways) for d in range(ways)])]
    all_gather x1, waiting for transfers between devices: 97.4 us -> 0.02 us  [local(): lax.all_gather(expand_weight, 'fsdp', axis=0, tiled=True)]
    all_gather x1, waiting for transfers between devices: 93.2 us -> 0.02 us  [local(): lax.all_gather(reduce_weight, 'fsdp', axis=0, tiled=True)]
    all_gather x1, waiting for transfers between devices: 70.6 us -> 0.02 us  [local(): lax.all_gather(projection_weight, 'fsdp', axis=0, tiled=True)]
    reduce_scatter x1, waiting for transfers between devices: 46.8 us -> 109 us  [local(): lax.psum_scatter(local_exp_w.astype(jnp.bfloat16), 'fsdp', scatter_dimens...]
    reduce_scatter x1, waiting for transfers between devices: 108 us -> 45.9 us  [local(): lax.psum_scatter(local_red_w.astype(jnp.bfloat16), 'fsdp', scatter_dimens...]
    all_gather x1, waiting for transfers between devices: 25.5 us -> 0.02 us  [local(): lax.all_gather(output_weight, 'fsdp', axis=0, tiled=True)]
  transfers between devices with their start and end apart: 18 -> 21, of which waited for: 16 -> 15; matrix products, arithmetic and copies ran while one was open for 11% -> 10% of each run, Pallas kernels for 0% -> 0%
where the time goes in v1:
time: 1780 us
  waiting for transfers between devices  948 us (53%)
  blocking collectives  596 us (33%)
  matrix products  89.9 us (5%)
  local copies, waits for them, and re-layouts  85 us (5%)
  other arithmetic  25.4 us (1%)
  between operations  21.4 us (1%)
    unnamed x2, blocking collectives  553 us
    ppermute x3, waiting for transfers between devices, doubled_up(): lax.ppermute(line, axis, [(d, (d - have) % ways) for d in range(ways)])  189 us
    reduce_scatter x1, waiting for transfers between devices, local(): lax.psum_scatter(local_mod_w.astype(jnp.bfloat16), 'fsdp', scatter_dimens...  158 us
    unnamed x23, waiting for transfers between devices  145 us
    reduce_scatter x1, waiting for transfers between devices, local(): lax.psum_scatter(local_exp_w.astype(jnp.bfloat16), 'fsdp', scatter_dimens...  109 us
    all_gather x1, waiting for transfers between devices, local(): lax.all_gather(modulation_weight, 'fsdp', axis=0, tiled=True)  108 us
    reduce_scatter x1, waiting for transfers between devices, local(): lax.psum_scatter(local_proj_w.astype(jnp.bfloat16), 'fsdp', scatter_dimen...  84.7 us
    unnamed x125, local copies, waits for them, and re-layouts  57.9 us
  transfers between devices with their start and end apart: 21, of which 15 were waited for; matrix products, arithmetic and copies ran while one was open for 10% of the time, Pallas kernels for 0%

profile of v1, /device:TPU:0, one launch (start us, length us, event | category | flops | bytes accessed | tf_op | source)
XLA Modules:
  0.0 1775.8 jit_solution(13372790501989748450)
XLA Ops:
  11.1 4.5 collective-permute-start
  15.6 56.1 %collective-permute-done = bf16[144,6912]{1,0:T(8,128)(2,1)S(1)} collective-permute-done((bf16[144,6912]{1,0:T(8,128)(2,1)S(1)}, bf16[144,6912]{1,0:T(8,128)(2,1)S(1)}, u32[]{:S(2)}, u32[]{:S(2)}) %collective-permute-start) | collective-permute-done | bytes 1990688 | tf_op jit(solution)/shard_map/ppermute | solution.py:15
  74.4 132.6 %collective-permute-done.1 = bf16[288,6912]{1,0:T(8,128)(2,1)} collective-permute-done((bf16[288,6912]{1,0:T(8,128)(2,1)}, bf16[288,6912]{1,0:T(8,128)(2,1)}, u32[]{:S(2)}, u32[]{:S(2)}) %collective-permute-start.1) | collective-permute-done | bytes 3981344 | tf_op jit(solution)/shard_map/ppermute | solution.py:15
  207.0 6.4 pad_maximum_fusion
  213.5 3.4 collective-permute-start.2
  222.0 524.5 %all-reduce.12 = (bf16[2304]{0:T(1024)(128)(2,1)S(1)}, bf16[6912]{0:T(1024)(128)(2,1)S(1)}, bf16[4608]{0:T(1024)(128)(2,1)S(1)}, bf16[1152]{0:T(1024)(128)(2,1)S(1)}, bf16[1152]{0:T(1024)(128)(2,1)}) all-reduce(bf16[2304]{0:T(1024)(128)(2,1)S(1)} %dynamic-update-slice.1, ...), channel_id=1, replica_groups=mesh['replica'=4,'fsdp'=8] {'fsdp'}, use_global_device_ids=true, to_apply=%add.1 | all-reduce | flops 16128 | bytes 64512
  753.5 4.3 constant_dynamic-update-slice_fusion.5
  757.8 7.0 constant_dynamic-update-slice_fusion.4
  767.6 4.3 constant_dynamic-update-slice_fusion.1
  771.9 6.9 constant_dynamic-update-slice_fusion
  778.8 9.3 fusion.12
  788.3 4.7 fusion.71
  794.8 3.3 fusion.78
  798.3 6.0 convolution_add_fusion
  805.8 5.8 convolution_convert_fusion
  811.7 8.6 fusion.83
  821.4 5.7 convolution_convert_fusion.1
  827.8 8.0 fusion.30
  845.0 5.9 fusion.82
  851.3 7.8 fusion.29
  860.8 6.0 multiply_convert_fusion
  870.6 6.6 convolution_convert_fusion.2
  877.3 45.9 %reduce-scatter.29.cloned.1.call-done = bf16[576,1152]{1,0:T(8,128)(2,1)} async-done(((bf16[4608,1152]{1,0:T(8,128)(2,1)}), bf16[576,1152]{1,0:T(8,128)(2,1)}) %reduce-scatter.29.cloned.1.call-update) | async-done | bytes 1327120 | tf_op jit(solution)/shard_map/reduce_scatter | solution.py:161
  923.2 2.6 copy.86
  925.9 108.7 %reduce-scatter.27.cloned.1.call-done = bf16[144,4608]{1,0:T(8,128)(2,1)} async-done(((bf16[1152,4608]{1,0:T(8,128)(2,1)}), bf16[144,4608]{1,0:T(8,128)(2,1)}) %reduce-scatter.27.cloned.1.call-update) | async-done | bytes 1327120 | tf_op jit(solution)/shard_map/reduce_scatter | solution.py:167
  1034.5 3.8 copy.84
  1038.4 157.7 %reduce-scatter.21.cloned.1.call-done = bf16[144,6912]{1,0:T(8,128)(2,1)} async-done(((bf16[1152,6912]{1,0:T(8,128)(2,1)}), bf16[144,6912]{1,0:T(8,128)(2,1)}) %reduce-scatter.21.cloned.1.call-update) | async-done | bytes 1990672 | tf_op jit(solution)/shard_map/reduce_scatter | solution.py:246
  1196.0 4.5 copy.78
  1200.6 34.5 %reduce-scatter.25.cloned.1.call-done = bf16[144,1152]{1,0:T(8,128)(2,1)} async-done(((bf16[1152,1152]{1,0:T(8,128)(2,1)}), bf16[144,1152]{1,0:T(8,128)(2,1)}) %reduce-scatter.25.cloned.1.call-update) | async-done | bytes 331792 | tf_op jit(solution)/shard_map/reduce_scatter | solution.py:258
  1237.8 84.7 %reduce-scatter.23.cloned.1.call-done = bf16[144,3456]{1,0:T(8,128)(2,1)} async-done(((bf16[1152,3456]{1,0:T(8,128)(2,1)}), bf16[144,3456]{1,0:T(8,128)(2,1)}) %reduce-scatter.23.cloned.1.call-update) | async-done | bytes 995344 | tf_op jit(solution)/shard_map/reduce_scatter | solution.py:252
  1322.5 2.6 copy.80
  1325.2 28.9 %reduce-scatter.39.cloned.1.call-done = bf16[288,576]{1,0:T(8,128)(2,1)} async-done(((bf16[1152,576]{1,0:T(8,128)(2,1)}), bf16[288,576]{1,0:T(8,128)(2,1)}) %reduce-scatter.39.cloned.1.call-update) | async-done | bytes 331792
  1354.1 41.3 %reduce-scatter.37.cloned.1.call-done = bf16[1152,144]{1,0:T(8,128)(2,1)} async-done(((bf16[4608,144]{1,0:T(8,128)(2,1)}), bf16[1152,144]{1,0:T(8,128)(2,1)}) %reduce-scatter.37.cloned.1.call-update) | async-done | bytes 331792
  1397.5 49.0 %reduce-scatter.31.cloned.1.call-done = bf16[1728,144]{1,0:T(8,128)(2,1)} async-done(((bf16[6912,144]{1,0:T(8,128)(2,1)}), bf16[1728,144]{1,0:T(8,128)(2,1)}) %reduce-scatter.31.cloned.1.call-update) | async-done | bytes 497680
  1456.0 29.0 %all-reduce.11 = (bf16[6912]{0:T(1024)(128)(2,1)S(1)}, bf16[2304]{0:T(1024)(128)(2,1)S(1)}, bf16[1152]{0:T(1024)(128)(2,1)S(1)}, bf16[4608]{0:T(1024)(128)(2,1)S(1)}, bf16[1152]{0:T(1024)(128)(2,1)S(1)}) all-reduce(bf16[6912]{0:T(1024)(128)(2,1)S(1)} %dynamic-update-slice.10, ...), channel_id=4, replica_groups=mesh['replica'=4,'fsdp'=8] {'fsdp'}, use_global_device_ids=true, to_apply=%region_21.23.clone | all-reduce | flops 16128 | bytes 64512
  1485.3 15.6 all-reduce.10
  1501.9 9.7 all-gather.2
  1513.0 107.9 %all-gather.20.cloned.1.call-done = bf16[1152,6912]{1,0:T(8,128)(2,1)} async-done(((bf16[144,6912]{1,0:T(8,128)(2,1)}), bf16[1152,6912]{1,0:T(8,128)(2,1)}) %all-gather.20.cloned.1.call-update) | async-done | bytes 15925264 | tf_op jit(solution)/shard_map/all_gather | solution.py:144
  1620.9 10.3 fusion.55
  1631.2 23.8 %reduce-scatter.33.cloned.1.call-done = bf16[864,144]{1,0:T(8,128)(2,1)} async-done(((bf16[3456,144]{1,0:T(8,128)(2,1)}), bf16[864,144]{1,0:T(8,128)(2,1)}) %reduce-scatter.33.cloned.1.call-update) | async-done | bytes 248848
  1656.3 17.7 all-gather.1
  1676.7 12.7 all-gather.24.cloned.1.call-done
  1689.4 2.9 copy.73
  1692.3 28.3 %all-gather.22.cloned.1.call-done = bf16[144,4608]{1,0:T(8,128)(2,1)} async-done(((bf16[144,1152]{1,0:T(8,128)(2,1)}), bf16[144,4608]{1,0:T(8,128)(2,1)}) %all-gather.22.cloned.1.call-update) | async-done | bytes 1327120 | tf_op jit(solution)/shard_map/all_gather | solution.py:292
  1720.6 3.1 convert_element_type.254
  1723.7 34.3 %all-gather.26.cloned.1.call-done = bf16[4,1728,144]{1,2,0:T(8,128)(2,1)} async-done(((bf16[1,1728,144]{1,2,0:T(8,128)(2,1)}), bf16[4,1728,144]{1,2,0:T(8,128)(2,1)}) %all-gather.26.cloned.1.call-update) | async-done | bytes 1990672 | tf_op jit(solution)/shard_map/all_gather | solution.py:283
  1758.0 4.6 copy.69
  1762.6 5.9 reshape.550
  (229 shorter events, 56.8 us)
Async XLA Ops:
  7.2 3.9 copy-start
  7.2 781.1 %all-gather.12.cloned.1.call-start = ((), (), s32[]{:S(2)}) async-start(), calls=%async_computation.10 | async-start | bytes 8957952 | tf_op jit(solution)/shard_map/all_gather | solution.py:83
  9.5 738.0 %copy-start.4 = (bf16[1,256,1152]{2,1,0:T(8,128)(2,1)}, bf16[1,256,1152]{2,1,0:T(8,128)(2,1)S(1)}, u32[]{:S(2)}) copy-start(bf16[1,256,1152]{2,1,0:T(8,128)(2,1)S(1)} %copy.112) | copy-start | bytes 1769476
  9.5 785.3 %all-gather.14.cloned.1.call-start = ((), (), s32[]{:S(2)}) async-start(), calls=%async_computation.11 | async-start | bytes 2985984 | tf_op jit(solution)/shard_map/all_gather | solution.py:85
  10.3 788.0 %all-gather.16.cloned.1.call-start = ((), (), s32[]{:S(2)}) async-start(), calls=%async_computation.12 | async-start | bytes 11943936 | tf_op jit(solution)/shard_map/all_gather | solution.py:87
  11.0 800.7 %all-gather.18.cloned.1.call-start = ((), (), s32[]{:S(2)}) async-start(), calls=%async_computation.13 | async-start | bytes 11943936 | tf_op jit(solution)/shard_map/all_gather | solution.py:89
  11.1 60.6 %collective-permute-start = (bf16[144,6912]{1,0:T(8,128)(2,1)S(1)}, bf16[144,6912]{1,0:T(8,128)(2,1)S(1)}, u32[]{:S(2)}, u32[]{:S(2)}) collective-permute-start(bf16[144,6912]{1,0:T(8,128)(2,1)S(1)} %copy-done), channel_id=1, source_target_pairs={{0,7},{1,0},{2,1},{3,2},{4,3},{5,4},{6,5},{7,6},{8,15},{9,8},{10,9... | collective-permute-start | bytes 5971976 | tf_op jit(solution)/shard_map/ppermute | solution.py:15
  74.3 132.8 %collective-permute-start.1 = (bf16[288,6912]{1,0:T(8,128)(2,1)}, bf16[288,6912]{1,0:T(8,128)(2,1)}, u32[]{:S(2)}, u32[]{:S(2)}) collective-permute-start(bf16[288,6912]{1,0:T(8,128)(2,1)} %pad_maximum_fusion.1), channel_id=1, source_target_pairs={{0,6},{1,7},{2,0},{3,1},{4,2},{5,3},{6,4},{7,5},{8,14},{9,15},{10,... | collective-permute-start | bytes 11943944 | tf_op jit(solution)/shard_map/ppermute | solution.py:15
  74.3 143.2 %copy-start.32 = (u32[32]{0:T(128)S(1)}, u32[32]{0:T(128)}, u32[]{:S(2)}) copy-start(u32[32]{0:T(128)} %constant.125) | copy-start | bytes 388
  74.3 146.4 %copy-start.41 = (bf16[144]{0:T(256)(128)(2,1)S(1)}, bf16[144]{0:T(256)(128)(2,1)}, u32[]{:S(2)}) copy-start(bf16[144]{0:T(256)(128)(2,1)} %param.26) | copy-start | bytes 868
  74.3 146.7 %copy-start.42 = (bf16[144]{0:T(256)(128)(2,1)S(1)}, bf16[144]{0:T(256)(128)(2,1)}, u32[]{:S(2)}) copy-start(bf16[144]{0:T(256)(128)(2,1)} %param.30) | copy-start | bytes 868
  74.3 146.9 %copy-start.33 = (bf16[864]{0:T(1024)(128)(2,1)S(1)}, bf16[864]{0:T(1024)(128)(2,1)}, u32[]{:S(2)}) copy-start(bf16[864]{0:T(1024)(128)(2,1)} %param.22) | copy-start | bytes 5188
  74.3 147.2 %copy-start.34 = (bf16[576]{0:T(1024)(128)(2,1)S(1)}, bf16[576]{0:T(1024)(128)(2,1)}, u32[]{:S(2)}) copy-start(bf16[576]{0:T(1024)(128)(2,1)} %param.28) | copy-start | bytes 3460
  74.3 147.4 %copy-start.37 = (bf16[288]{0:T(512)(128)(2,1)S(1)}, bf16[288]{0:T(512)(128)(2,1)}, u32[]{:S(2)}) copy-start(bf16[288]{0:T(512)(128)(2,1)} %param.24) | copy-start | bytes 1732
  74.4 672.2 %copy-start.43 = (s32[1,128]{1,0:T(1,128)S(1)}, s32[1,128]{1,0:T(1,128)}, u32[]{:S(2)}) copy-start(s32[1,128]{1,0:T(1,128)} %param.20) | copy-start | bytes 1540
  74.4 848.8 %reduce-scatter.29.cloned.1.call-start = ((), (), s32[]{:S(2)}) async-start(), calls=%async_computation.20 | async-start | bytes 11943936 | tf_op jit(solution)/shard_map/reduce_scatter | solution.py:161
  213.5 544.3 %collective-permute-start.2 = (bf16[576,6912]{1,0:T(8,128)(2,1)}, bf16[576,6912]{1,0:T(8,128)(2,1)}, u32[]{:S(2)}, u32[]{:S(2)}) collective-permute-start(bf16[576,6912]{1,0:T(8,128)(2,1)} %pad_maximum_fusion), channel_id=1, source_target_pairs={{0,4},{1,5},{2,6},{3,7},{4,0},{5,1},{6,2},{7,3},{8,12},{9,13},{10,... | collective-permute-start | bytes 23887880 | tf_op jit(solution)/shard_map/ppermute | solution.py:15
  746.6 4.0 copy-start.28
  749.6 62.1 %copy-start.29 = (f32[128]{0:T(128)}, f32[128]{0:T(128)S(1)}, u32[]{:S(2)}) copy-start(f32[128]{0:T(128)S(1)} %fusion.68) | copy-start | bytes 1540
  794.7 3.5 copy-start.13
  798.3 7.5 copy-start.12
  811.6 222.9 %reduce-scatter.27.cloned.1.call-start = ((), (), s32[]{:S(2)}) async-start(), calls=%async_computation.18 | async-start | bytes 11943936 | tf_op jit(solution)/shard_map/reduce_scatter | solution.py:167
  827.1 368.9 %reduce-scatter.21.cloned.1.call-start = ((), (), s32[]{:S(2)}) async-start(), calls=%async_computation.15 | async-start | bytes 17915904 | tf_op jit(solution)/shard_map/reduce_scatter | solution.py:246
  827.8 9.1 copy-start.30
  836.1 5.3 copy-start.35
  843.9 7.1 copy-start.26
  844.4 6.6 copy-start.27
  845.0 6.0 copy-start.24
  845.0 6.3 copy-start.10
  845.0 6.3 copy-start.36
  851.0 8.1 copy-start.23
  851.3 7.8 copy-start.39
  866.9 3.7 copy-start.25
  866.9 368.3 %reduce-scatter.25.cloned.1.call-start = ((), (), s32[]{:S(2)}) async-start(), calls=%async_computation.17 | async-start | bytes 2985984 | tf_op jit(solution)/shard_map/reduce_scatter | solution.py:258
  870.2 452.3 %reduce-scatter.23.cloned.1.call-start = ((), (), s32[]{:S(2)}) async-start(), calls=%async_computation.16 | async-start | bytes 8957952 | tf_op jit(solution)/shard_map/reduce_scatter | solution.py:252
  877.2 476.8 %reduce-scatter.39.cloned.1.call-start = ((), (), s32[]{:S(2)}) async-start(), calls=%async_computation.27 | async-start | bytes 1843200
  925.8 469.6 %reduce-scatter.37.cloned.1.call-start = ((), (), s32[]{:S(2)}) async-start(), calls=%async_computation.26 | async-start | bytes 2949120
  1038.3 408.1 %reduce-scatter.31.cloned.1.call-start = ((), (), s32[]{:S(2)}) async-start(), calls=%async_computation.23 | async-start | bytes 4423680
  1200.6 300.3 %reduce-scatter.35.cloned.1.call-start = ((), (), s32[]{:S(2)}) async-start(), calls=%async_computation.25 | async-start | bytes 737280
  1237.2 383.7 %all-gather.20.cloned.1.call-start = ((), (), s32[]{:S(2)}) async-start(), calls=%async_computation.14 | async-start | bytes 17915904 | tf_op jit(solution)/shard_map/all_gather | solution.py:144
  1237.8 417.3 %reduce-scatter.33.cloned.1.call-start = ((), (), s32[]{:S(2)}) async-start(), calls=%async_computation.24 | async-start | bytes 2211840
  1325.1 126.2 %copy-start.44 = (s32[1,128]{1,0:T(1,128)S(1)}, s32[1,128]{1,0:T(1,128)}, u32[]{:S(2)}) copy-start(s32[1,128]{1,0:T(1,128)} %param.20) | copy-start | bytes 1540
  1325.1 126.5 %copy-start.5 = (bf16[1,256,1152]{2,1,0:T(8,128)(2,1)S(1)}, bf16[1,256,1152]{2,1,0:T(8,128)(2,1)}, u32[]{:S(2)}) copy-start(bf16[1,256,1152]{2,1,0:T(8,128)(2,1)} %copy-done.4) | copy-start | bytes 1769476
  1325.1 364.3 %all-gather.24.cloned.1.call-start = ((), (), s32[]{:S(2)}) async-start(), calls=%async_computation.21 | async-start | bytes 1843200 | tf_op jit(solution)/shard_map/all_gather | solution.py:295
  1354.1 366.5 %all-gather.22.cloned.1.call-start = ((), (), s32[]{:S(2)}) async-start(), calls=%async_computation.19 | async-start | bytes 1658880 | tf_op jit(solution)/shard_map/all_gather | solution.py:292
  1397.4 360.5 %all-gather.26.cloned.1.call-start = ((), (), s32[]{:S(2)}) async-start(), calls=%async_computation.22 | async-start | bytes 2580480 | tf_op jit(solution)/shard_map/all_gather | solution.py:283
  1453.9 59.1 %copy-start.6 = (bf16[256,1152]{1,0:T(8,128)(2,1)}, bf16[256,1152]{1,0:T(8,128)(2,1)S(1)}, u32[]{:S(2)}) copy-start(bf16[256,1152]{1,0:T(8,128)(2,1)S(1)} %scatter_custom_fusion.1) | copy-start | bytes 1769476
  1455.9 175.3 %copy-start.3 = (bf16[256,1152]{1,0:T(8,128)(2,1)}, bf16[256,1152]{1,0:T(8,128)(2,1)S(1)}, u32[]{:S(2)}) copy-start(bf16[256,1152]{1,0:T(8,128)(2,1)S(1)} %scatter_custom_fusion) | copy-start | bytes 1769476
  (18 other events, 23.0 us)
Sparse Core Ops, SparseCore 0:
  9.7 111.6 all-gather.11
  123.0 54.4 all-gather.13
  179.2 341.6 all-gather.15
  522.3 141.4 all-gather.17
  811.8 111.3 reduce-scatter.28
  925.5 109.0 reduce-scatter.26
  1036.9 159.0 reduce-scatter.20
  1199.0 36.0 reduce-scatter.24
  1237.6 84.9 reduce-scatter.22
  1325.3 28.6 reduce-scatter.38
  1358.0 37.3 reduce-scatter.36
  1399.2 47.1 reduce-scatter.30
  1450.1 25.0 reduce-scatter.34
  1476.7 144.1 all-gather.19
  1624.3 30.6 reduce-scatter.32
  1656.8 32.5 all-gather.23
  1691.6 28.9 all-gather.21
  1722.9 35.0 all-gather.25
